TPU v7x, 32 devices: a whole 2x2x4 slice. The times are simulated.
32 devices in a mesh: pose: 4 (over y, core), slab: 8 (over z, x).
Axes of the slice: x: 2, y: 2, z: 4, core: 2. Of those that a mesh axis runs over, the one named last changes fastest.
Arguments:
- coords: float32 [4, 3, 2048], P('pose'), may hold values from -12 to 12, as said below
- atom_types: int32 [4, 2048], P('pose'), may hold values from 0 to 27
- counts: int32 [4], P('pose'), may hold values from 1024 to 2048, as said below
- labels: int32 [4], P('pose'), may hold values from 0 to 1
- receptor_density: bfloat16 [4, 28, 16, 4096], P('pose', None, 'slab'), may hold values from 0 to 1.5
- type_radii: float32 [28], replicated, may hold values from 1.2 to 2.2
- w_stem: bfloat16 [32, 28, 3, 3, 3], replicated, may hold values from -1.25 to 1.25
- w_one: bfloat16 [32, 32, 3, 3, 3], replicated, may hold values from -0.21875 to 0.21875
- w_two: bfloat16 [32, 32, 3, 3, 3], replicated, may hold values from -0.21875 to 0.21875
- w_head: float32 [32], replicated, may hold values from -8 to 8
Outputs:
- scores: float32 [4], P('pose')
- pose_loss: float32 [4], P('pose')
- atom_grad: float32 [4, 3, 2048], P('pose')
- grad_stem: float32 [32, 28, 3, 3, 3], replicated
- grad_one: float32 [32, 32, 3, 3, 3], replicated
- grad_two: float32 [32, 32, 3, 3, 3], replicated
- grad_head: float32 [32], replicated
Inputs may be any that keep to these rules, and one draw needn't show every extreme that they name: The live atoms of a pose are the first counts[p] slots; every pose has 1024 or more of them, and some pose has all 2048. `coords`: every atom lies inside the box of the grid, 0.75 or more from its faces.
All inputs are finite; a program needn't handle non-finite values.
Results may differ from a plain program's by a relative error of at most 0.005.
The roundings to bfloat16 on the way count: a program that leaves them out, or rounds other values in their place, can miss the bound.
Values may be sent and summed in bfloat16 or wider, within the bound.
No kernel may reach another device: no remote copies, remote signals or barrier semaphores. Data moves between devices by JAX's collectives and lax.ppermute only.
A program may use at most 256 MiB of HBM per device.

v0:
```python
import jax
import jax.numpy as jnp
from jax import lax
from jax.sharding import PartitionSpec as P

NXY = 64
CZ = 2
resolution = 0.375
conv_dims = ("NCDHW", "OIDHW", "NCDHW")
grad_dims = ("CNDHW", "IODHW", "NCDHW")


def extended(cells, sides, width):
    for axis, dim in sides:
        count = lax.axis_size(axis)
        ends = count - 1
        head = lax.slice_in_dim(cells, 0, width, axis=dim)
        tail = lax.slice_in_dim(cells, cells.shape[dim] - width, cells.shape[dim], axis=dim)
        cells = jnp.concatenate(
            [
                lax.ppermute(tail, axis, [(i, (i + 1) % count) for i in range(ends)]),
                cells,
                lax.ppermute(head, axis, [((i + 1) % count, i) for i in range(ends)]),
            ],
            axis=dim,
        )
    return cells


def gauss_table(centres, places, inv_sq):
    offset = centres[None, :, None] - places[:, None, :]
    bumps = jnp.exp(-2.0 * offset * offset * inv_sq[:, None, :])
    return (bumps, 4.0 * offset * inv_sq[:, None, :] * bumps)


def spatial(volume):
    return volume.reshape(volume.shape[0], volume.shape[1], volume.shape[2], NXY, NXY)


def flatten(volume):
    return volume.reshape(volume.shape[0], volume.shape[1], volume.shape[2], NXY * NXY)


def conv_valid(padded, kernel):
    result = lax.conv_general_dilated(
        spatial(padded),
        kernel,
        (1, 1, 1),
        [(0, 0), (1, 1), (1, 1)],
        dimension_numbers=conv_dims,
        preferred_element_type=jnp.float32,
    )
    return flatten(result)


def flipped(kernel):
    return jnp.flip(kernel, (2, 3, 4)).transpose(1, 0, 2, 3, 4)


def kernel_grad(padded, upstream):
    result = lax.conv_general_dilated(
        spatial(padded),
        spatial(upstream),
        (1, 1, 1),
        [(0, 0), (1, 1), (1, 1)],
        dimension_numbers=grad_dims,
        preferred_element_type=jnp.float32,
    )
    return result.transpose(1, 0, 2, 3, 4)


def with_rims(volume):
    return extended(volume, (("slab", 2),), 1)


def to_grid(row_cols, plane_count, type_count):
    pose_count = row_cols.shape[0]
    volume = row_cols.reshape(pose_count, plane_count, NXY, type_count, NXY).transpose(
        0, 3, 1, 2, 4
    )
    return volume.reshape(pose_count, type_count, plane_count, NXY * NXY)


def local(
    coords, atom_types, counts, labels, receptor_density, type_radii, w_stem, w_one, w_two, w_head
):
    pose_count = coords.shape[0]
    atom_count = coords.shape[2]
    type_count = type_radii.shape[0]
    slab_count = lax.axis_size("slab")
    total_depth = CZ * slab_count
    cell_count = total_depth * NXY * NXY
    start_plane = lax.axis_index("slab") * CZ
    highest = lax.Precision.HIGHEST
    centres_xy = (jnp.arange(NXY, dtype=jnp.float32) + 0.5 - 0.5 * NXY) * resolution
    kind_ids = jnp.arange(type_count, dtype=jnp.int32)
    type_hits = (atom_types[:, None, :] == kind_ids[None, :, None]).astype(jnp.float32)
    alive = (jnp.arange(atom_count, dtype=jnp.int32)[None, :] < counts[:, None]).astype(jnp.float32)
    live_types = type_hits * alive[:, None, :]
    radius = jnp.sum(type_hits * type_radii[None, :, None], axis=1)
    inv_sq = 1.0 / (radius * radius)
    gauss_x, slope_x = gauss_table(centres_xy, coords[:, 0], inv_sq)
    gauss_y, slope_y = gauss_table(centres_xy, coords[:, 1], inv_sq)
    across_table = (
        (live_types[:, :, None, :] * gauss_y[:, None])
        .reshape(pose_count, type_count * NXY, atom_count)
        .astype(jnp.bfloat16)
    )
    slope_table = (
        (live_types[:, :, None, :] * slope_y[:, None])
        .reshape(pose_count, type_count * NXY, atom_count)
        .astype(jnp.bfloat16)
    )
    plane_count = CZ + 2 * 0
    planes = start_plane - 0 + jnp.arange(plane_count, dtype=jnp.int32)
    inside = ((planes >= 0) & (planes < total_depth)).astype(jnp.float32)
    centres_z = (planes.astype(jnp.float32) + 0.5 - 0.5 * total_depth) * resolution
    gauss_z, slope_z = gauss_table(centres_z, coords[:, 2], inv_sq)
    gauss_z = gauss_z * inside[None, :, None]
    depth_table = (
        (gauss_z[:, :, None, :] * gauss_x[:, None])
        .reshape(pose_count, plane_count * NXY, atom_count)
        .astype(jnp.bfloat16)
    )
    row_cols = jnp.einsum(
        "pra,pqa->prq", depth_table, across_table, preferred_element_type=jnp.float32
    )
    splat, gauss_z, slope_z, inside = (
        to_grid(row_cols, plane_count, type_count),
        gauss_z,
        slope_z,
        inside,
    )
    density = (splat + receptor_density.astype(jnp.float32)).astype(jnp.bfloat16)
    density_pad = with_rims(density)
    stem_pre = conv_valid(density_pad, w_stem)
    hidden_one = jnp.maximum(stem_pre, 0.0).astype(jnp.bfloat16)
    hidden_pad = with_rims(hidden_one)
    second_pre = conv_valid(hidden_pad, w_one)
    hidden_two = jnp.maximum(second_pre, 0.0).astype(jnp.bfloat16)
    two_pad = with_rims(hidden_two)
    summed = hidden_one.astype(jnp.float32) + conv_valid(two_pad, w_two)
    part_pool = jnp.sum(jnp.maximum(summed, 0.0), axis=(2, 3)) / cell_count
    pooled = lax.psum(part_pool, "slab")
    scores = jnp.sum(pooled * w_head[None, :], axis=1)
    label_sign = (2 * labels - 1).astype(jnp.float32)
    pose_loss = jax.nn.softplus(-label_sign * scores)
    score_grad = -label_sign * jax.nn.sigmoid(-label_sign * scores)
    head_term = jnp.sum(score_grad[:, None] * part_pool, axis=0)
    top_grad = jnp.where(
        summed > 0, (score_grad[:, None] * w_head[None, :])[:, :, None, None], 0.0
    ).astype(jnp.bfloat16)
    grad_two_local = kernel_grad(two_pad, top_grad) / cell_count
    back_two = conv_valid(with_rims(top_grad), flipped(w_two))
    mid_grad = jnp.where(second_pre > 0, back_two, 0.0).astype(jnp.bfloat16)
    grad_one_local = kernel_grad(hidden_pad, mid_grad) / cell_count
    back_one = top_grad.astype(jnp.float32) + conv_valid(with_rims(mid_grad), flipped(w_one))
    stem_grad = jnp.where(stem_pre > 0, back_one, 0.0).astype(jnp.bfloat16)
    grad_stem_local = kernel_grad(density_pad, stem_grad) / cell_count
    density_grad = conv_valid(with_rims(stem_grad), flipped(w_stem)).astype(jnp.bfloat16)
    grid_rows = (
        density_grad.reshape(pose_count, type_count, CZ, NXY, NXY)
        .transpose(0, 2, 3, 1, 4)
        .reshape(pose_count, CZ * NXY, type_count * NXY)
    )
    rows_plain = jnp.einsum(
        "prq,pqa->pra", grid_rows, across_table, preferred_element_type=jnp.float32
    ).reshape(pose_count, CZ, NXY, atom_count)
    rows_slope = jnp.einsum(
        "prq,pqa->pra", grid_rows, slope_table, preferred_element_type=jnp.float32
    ).reshape(pose_count, CZ, NXY, atom_count)
    along_x = jnp.einsum("pzxa,pza,pxa->pa", rows_plain, gauss_z, slope_x, precision=highest)
    along_y = jnp.einsum("pzxa,pza,pxa->pa", rows_slope, gauss_z, gauss_x, precision=highest)
    along_z = jnp.einsum("pzxa,pza,pxa->pa", rows_plain, slope_z, gauss_x, precision=highest)
    local_force = jnp.stack([along_x, along_y, along_z], axis=1)
    atom_grad = lax.psum(local_force, "slab")
    grad_stem, grad_one, grad_two, grad_head = lax.psum(
        (grad_stem_local, grad_one_local, grad_two_local, head_term), ("pose", "slab")
    )
    return (scores, pose_loss, atom_grad, grad_stem, grad_one, grad_two, grad_head)


def solution(mesh):
    return jax.shard_map(
        local,
        mesh=mesh,
        in_specs=(
            P("pose", None, None),
            P("pose", None),
            P("pose"),
            P("pose"),
            P("pose", None, "slab", None),
            P(),
            P(),
            P(),
            P(),
            P(),
        ),
        out_specs=(P("pose"), P("pose"), P("pose", None, None), P(), P(), P(), P()),
        check_vma=False,
    )
```

profile of v0, /device:TPU:0, one launch (start us, length us, event | category | flops | bytes accessed | tf_op | source)
XLA Modules:
  0.0 759.1 jit_solution(6189887699078458096)
XLA Ops:
  22.2 6.3 collective-permute-start
  28.5 10.0 %multiply_convert_fusion = (bf16[28,64,2048]{2,1,0:T(8,128)(2,1)}, bf16[28,64,2048]{2,1,0:T(8,128)(2,1)}) fusion(f32[64,2048]{1,0:T(8,128)S(1)} %get-tuple-element.100, f32[28,2048]{1,0:T(8,128)S(1)} %fusion.158, f32[64,2048]{1,0:T(8,128)S(1)} %get-tuple-element.101), kind=kLoop, calls=%fused_computation | loop fusion | flops 14680064 | bytes 15958016 | tf_op jit(solution)/shard_map/convert_element_type | solution.py:112
  62.9 8.6 %copy.334 = bf16[28,4,64,1,8,9]{0,4,5,2,1,3:T(8,128)(2,1)} copy(bf16[28,4,64,1,8,9]{2,1,5,4,0,3:T(4,128)(2,1)} %bitcast.277) | data formatting | bytes 2064384 | tf_op jit(solution)/shard_map/conv_general_dilated | solution.py:45
  73.1 11.6 %maximum_convert_fusion.1 = (bf16[2,64,8,9,32]{4,2,3,1,0:T(8,128)(2,1)}, f32[2,64,8,9,32]{4,2,3,1,0:T(8,128)}) fusion(pred[8,9]{0,1:T(8,128)(4,1)S(1)} %copy-done.10, bf16[32,28,3,3,3]{1,0,4,3,2:T(8,128)(2,1)S(1)} %copy-done.13, bf16[28,4,64,1,7,2]{0,4,5,2,1,3:T(8,128)(2,1)S(1)} %slice.89, bf16[28,4,64,1,8,9]{0,4,5,2,1,3:T(8,128)(2,1)} %copy.334), kind=kOutput, calls=%fused_computation.94 | convolution fusion | flops 446226432 | bytes 3050824 | tf_op jit(solution)/shard_map/conv_general_dilated | solution.py:45
  97.8 5.8 collective-permute-start.2
  105.7 8.1 %copy.434 = bf16[28,4,64,1,8,8]{0,4,5,2,1,3:T(8,128)(2,1)} copy(bf16[28,4,64,1,8,8]{2,1,5,4,0,3:T(4,128)(2,1)} %get-tuple-element.78) | data formatting | bytes 1835008
  113.9 7.7 %copy.433 = bf16[28,4,64,1,8,8]{0,4,5,2,1,3:T(8,128)(2,1)} copy(bf16[28,4,64,1,8,8]{2,1,5,4,0,3:T(4,128)(2,1)} %get-tuple-element.77) | data formatting | bytes 1835008
  122.7 9.0 %fusion.75 = (bf16[28,4,64,8,9,1]{0,3,5,4,2,1:T(8,128)(2,1)}, bf16[28,4,64,8,9,1]{0,3,5,4,2,1:T(8,128)(2,1)}) fusion(bf16[28,4,64,1,7,1]{0,4,5,2,1,3:T(8,128)(2,1)} %copy.435, bf16[28,4,64,1,8,8]{0,4,5,2,1,3:T(8,128)(2,1)} %copy.434, bf16[28,4,64,1,8,8]{0,4,5,2,1,3:T(8,128)(2,1)} %copy.433, bf16[28,4,64,1,7,1]{0,4,5,2,1,3:T(8,128)(2,1)} %copy.432), kind=kLoop, calls=%fused_computation.77 | loop fusion | flops 6193152 | bytes 4100096 | tf_op jit(solution)/shard_map/reshape | solution.py:37
  131.7 6.8 copy.377
  149.3 6.7 copy.340
  157.5 10.4 %maximum_convert_fusion = (bf16[2,64,8,9,32]{4,2,3,1,0:T(8,128)(2,1)}, f32[2,64,8,9,32]{4,2,3,1,0:T(8,128)}) fusion(pred[8,9]{0,1:T(8,128)(4,1)S(1)} %copy-done.10, bf16[32,32,3,3,3]{1,0,4,3,2:T(8,128)(2,1)S(1)} %copy-done, bf16[32,4,64,1,7,2]{0,4,5,2,1,3:T(8,128)(2,1)S(1)} %slice.93, bf16[32,4,64,1,8,9]{0,4,5,2,1,3:T(8,128)(2,1)} %copy.340), kind=kOutput, calls=%fused_computation.92 | convolution fusion | flops 509804544 | bytes 3233864 | tf_op jit(solution)/shard_map/conv_general_dilated | solution.py:45
  188.3 7.7 %copy.437 = bf16[32,4,64,1,8,8]{0,4,5,2,1,3:T(8,128)(2,1)} copy(bf16[32,4,64,1,8,8]{2,0,5,4,1,3:T(8,128)(2,1)} %get-tuple-element.69) | data formatting | bytes 2097152
  197.0 7.6 %copy.438 = bf16[32,4,64,1,8,8]{0,4,5,2,1,3:T(8,128)(2,1)} copy(bf16[32,4,64,1,8,8]{2,0,5,4,1,3:T(8,128)(2,1)} %get-tuple-element.70) | data formatting | bytes 2097152
  204.7 8.8 %fusion.79 = (bf16[32,4,64,8,9,1]{0,3,5,4,2,1:T(8,128)(2,1)}, bf16[32,4,64,8,9,1]{0,3,5,4,2,1:T(8,128)(2,1)}) fusion(bf16[32,4,64,1,7,1]{0,4,5,2,1,3:T(8,128)(2,1)S(1)} %copy.436, bf16[32,4,64,1,8,8]{0,4,5,2,1,3:T(8,128)(2,1)} %copy.437, bf16[32,4,64,1,7,1]{0,4,5,2,1,3:T(8,128)(2,1)} %copy.439, bf16[32,4,64,1,8,8]{0,4,5,2,1,3:T(8,128)(2,1)} %copy.438), kind=kLoop, calls=%fused_computation.81 | loop fusion | flops 7077888 | bytes 4685824 | tf_op jit(solution)/shard_map/concatenate | solution.py:19
  213.4 5.5 copy.383
  227.5 6.8 copy.346
  235.8 11.3 %select_reduce_fusion = (f32[32]{0:T(128)S(1)}, f32[2,64,8,9,32]{4,2,3,1,0:T(8,128)}) fusion(bf16[2,64,8,9,32]{4,2,3,1,0:T(8,128)(2,1)} %get-tuple-element.109, pred[8,9]{0,1:T(8,128)(4,1)S(1)} %copy-done.10, bf16[32,32,3,3,3]{1,0,4,3,2:T(8,128)(2,1)S(1)} %copy-done.11, bf16[32,4,64,1,7,2]{0,4,5,2,1,3:T(8,128)(2,1)S(1)} %slice.97, ...), kind=kOutput, calls=%fused_computation.91 | convolution fusion | flops 510394336 | bytes 3233992 | tf_op jit(solution)/shard_map/conv_general_dilated | solution.py:45
  247.1 19.5 %psum.42 = f32[1,32]{1,0:T(1,128)S(1)} all-reduce(f32[1,32]{1,0:T(1,128)S(1)} %multiply_bitcast_fusion), channel_id=1, replica_groups=mesh['pose'=4,'slab'=8] {'slab'}, use_global_device_ids=true, to_apply=%region_2.0 | all-reduce | flops 32 | bytes 256 | tf_op jit(solution)/shard_map/psum | solution.py:144
  305.1 7.7 %copy.441 = bf16[32,4,64,1,8,8]{0,4,5,2,1,3:T(8,128)(2,1)} copy(bf16[32,4,64,1,8,8]{2,0,5,4,1,3:T(8,128)(2,1)} %get-tuple-element.65) | data formatting | bytes 2097152
  313.8 7.7 %copy.442 = bf16[32,4,64,1,8,8]{0,4,5,2,1,3:T(8,128)(2,1)} copy(bf16[32,4,64,1,8,8]{2,0,5,4,1,3:T(8,128)(2,1)} %get-tuple-element.66) | data formatting | bytes 2097152
  326.9 36.8 %psum.47 = f32[32]{0:T(128)} all-reduce(f32[32]{0:T(128)S(1)} %broadcast_multiply_fusion.2), channel_id=1, replica_groups=mesh['pose'=4,'slab'=8] {'pose','slab'}, use_global_device_ids=true, to_apply=%region_8.9 | all-reduce | flops 32 | bytes 256 | tf_op jit(solution)/shard_map/psum | solution.py:177
  363.7 9.1 %fusion.81 = (bf16[32,4,64,8,9,1]{0,3,5,4,2,1:T(8,128)(2,1)}, bf16[32,4,64,8,9,1]{0,3,5,4,2,1:T(8,128)(2,1)}) fusion(bf16[32,4,64,1,7,1]{0,4,5,2,1,3:T(8,128)(2,1)S(1)} %copy.440, bf16[32,4,64,1,8,8]{0,4,5,2,1,3:T(8,128)(2,1)} %copy.441, bf16[32,4,64,1,7,1]{0,4,5,2,1,3:T(8,128)(2,1)} %copy.443, bf16[32,4,64,1,8,8]{0,4,5,2,1,3:T(8,128)(2,1)} %copy.442), kind=kLoop, calls=%fused_computation.83 | loop fusion | flops 7077888 | bytes 4685824 | tf_op jit(solution)/shard_map/concatenate | solution.py:19
  372.8 22.9 %fusion.117 = f32[32,32,3,3,3]{0,1,4,3,2:T(8,128)} fusion(bf16[2,64,8,9,32]{4,2,3,1,0:T(8,128)(2,1)S(1)} %copy-done.1, pred[8,9]{0,1:T(8,128)(4,1)S(1)} %copy-done.10, bf16[32,4,64,8,9,1]{0,3,5,4,2,1:T(8,128)(2,1)} %get-tuple-element.121, bf16[32,4,64,8,9,1]{0,3,5,4,2,1:T(8,128)(2,1)} %copy.389, bf16[32,4,64,8,9,1]{0,3,5,4,2,1:T(8,128)(2,1)} %get-tuple-element.120), kind=kOutput, calls=%fused_computation.128 | convolution fusion | flops 515238912 | bytes 4239432 | tf_op jit(solution)/shard_map/transpose | solution.py:69
  408.2 12.1 %select_convert_fusion.1 = bf16[2,64,8,9,32]{4,2,3,1,0:T(8,128)(2,1)} fusion(f32[2,64,8,9,32]{4,2,3,1,0:T(8,128)} %get-tuple-element.112, pred[8,9]{0,1:T(8,128)(4,1)S(1)} %copy-done.10, bf16[32,32,3,3,3]{1,0,4,3,2:T(8,128)(2,1)S(1)} %copy-done.12, bf16[32,4,64,1,7,2]{0,4,5,2,1,3:T(8,128)(2,1)S(1)} %slice.103, bf16[32,4,64,1,8,9]{0,4,5,2,1,3:T(8,128)(2,1)} %copy.355), kind=kOutput, calls=%fused_computation.89 | convolution fusion | flops 510099456 | bytes 3233864 | tf_op jit(solution)/shard_map/conv_general_dilated | solution.py:45
  432.0 23.5 %fusion.127 = f32[32,32,3,3,3]{0,1,4,3,2:T(8,128)} fusion(bf16[2,64,8,9,32]{4,2,3,1,0:T(8,128)(2,1)} %select_convert_fusion.1, pred[8,9]{0,1:T(8,128)(4,1)S(1)} %copy-done.10, bf16[32,4,64,8,9,1]{0,3,5,4,2,1:T(8,128)(2,1)} %get-tuple-element.119, bf16[32,4,64,8,9,1]{0,3,5,4,2,1:T(8,128)(2,1)} %copy.383, bf16[32,4,64,8,9,1]{0,3,5,4,2,1:T(8,128)(2,1)} %get-tuple-element.118), kind=kOutput, calls=%fused_computation.130 | convolution fusion | flops 515238912 | bytes 4239432 | tf_op jit(solution)/shard_map/transpose | solution.py:69
  459.2 5.5 copy.361
  466.2 12.4 %select_convert_fusion = (bf16[2,64,8,9,32]{4,2,3,1,0:T(8,128)(2,1)}, pred[2,64,8,9,32]{4,2,3,1,0:T(8,128)(4,1)S(1)}, f32[2,64,8,9,32]{4,2,3,1,0:T(8,128)}) fusion(bf16[2,64,8,9,32]{4,2,3,1,0:T(8,128)(2,1)} %select_convert_fusion.2, f32[2,64,8,9,32]{4,2,3,1,0:T(8,128)} %get-tuple-element.110, pred[8,9]{0,1:T(8,128)(4,1)S(1)} %copy-done.10, ...), kind=kOutput, calls=%fused_computation.88 | convolution fusion | flops 510689280 | bytes 5298248 | tf_op jit(solution)/shard_map/conv_general_dilated | solution.py:45
  498.5 5.6 collective-permute-start.10
  504.2 23.3 %fusion.137 = f32[32,28,3,3,3]{0,1,4,3,2:T(8,128)} fusion(bf16[2,64,8,9,32]{4,2,3,1,0:T(8,128)(2,1)} %get-tuple-element.63, pred[8,9]{0,1:T(8,128)(4,1)S(1)} %copy-done.10, bf16[28,4,64,8,9,1]{0,3,5,4,2,1:T(8,128)(2,1)} %get-tuple-element.116, bf16[28,4,64,8,9,1]{0,3,5,4,2,1:T(8,128)(2,1)} %copy.377, bf16[28,4,64,8,9,1]{0,3,5,4,2,1:T(8,128)(2,1)} %get-tuple-element.117), kind=kOutput, calls=%fused_computation.132 | convolution fusion | flops 450870912 | bytes 3783240 | tf_op jit(solution)/shard_map/transpose | solution.py:69
  527.6 134.7 %all-reduce.3.cloned.1.call-done = (f32[32,28,3,3,3]{0,1,4,3,2:T(8,128)}, f32[32,32,3,3,3]{0,1,4,3,2:T(8,128)}, f32[32,32,3,3,3]{0,1,4,3,2:T(8,128)}) async-done(((f32[32,28,3,3,3]{0,1,4,3,2:T(8,128)}, f32[32,32,3,3,3]{0,1,4,3,2:T(8,128)}, f32[32,32,3,3,3]{0,1,4,3,2:T(8,128)}), (f32[32,28,3,3,3]{0,1,4,3,2:T(8,128)}, f32[32,32,3,3,3]{0,1,4,3,2:T(8,128)}, ...) | async-done | bytes 317968 | tf_op jit(solution)/shard_map/psum | solution.py:177
  678.9 10.3 %fusion.54 = bf16[2,64,8,9,28]{4,2,3,1,0:T(8,128)(2,1)} fusion(bf16[32,28,3,3,3]{1,0,4,3,2:T(8,128)(2,1)S(1)} %copy-done.14, bf16[32,4,64,1,7,2]{0,4,5,2,1,3:T(8,128)(2,1)S(1)} %slice.112, bf16[32,4,64,1,8,9]{0,4,5,2,1,3:T(8,128)(2,1)} %copy.368), kind=kOutput, calls=%fused_computation.57 | convolution fusion | flops 445587456 | bytes 1973504 | tf_op jit(solution)/shard_map/conv_general_dilated | solution.py:45
  713.1 37.6 %psum.43 = f32[1,3,2048]{2,0,1:T(1,128)} all-reduce(f32[1,3,2048]{2,0,1:T(1,128)S(1)} %pad_maximum_fusion.1), channel_id=1, replica_groups=mesh['pose'=4,'slab'=8] {'slab'}, use_global_device_ids=true, to_apply=%region_4.5 | all-reduce | flops 6144 | bytes 49152 | tf_op jit(solution)/shard_map/psum | solution.py:176
  (183 shorter events, 233.2 us)
Async XLA Ops:
  7.2 150.3 %copy-start = (bf16[32,32,3,3,3]{1,0,4,3,2:T(8,128)(2,1)S(1)}, bf16[32,32,3,3,3]{1,0,4,3,2:T(8,128)(2,1)}, u32[]{:S(2)}) copy-start(bf16[32,32,3,3,3]{1,0,4,3,2:T(8,128)(2,1)} %param.17) | copy-start | bytes 165892
  7.2 655.1 %all-reduce.3.cloned.1.call-start = ((), (), s32[]{:S(2)}) async-start(), calls=%async_computation | async-start | bytes 2654208 | tf_op jit(solution)/shard_map/psum | solution.py:177
  11.9 7.0 copy-start.9
  20.9 21.1 %collective-permute-start.1 = (bf16[1,28,1,4096]{3,2,1,0:T(2,128)(2,1)S(1)}, bf16[1,28,1,4096]{3,2,1,0:T(2,128)(2,1)S(1)}, u32[]{:S(2)}, u32[]{:S(2)}) collective-permute-start(bf16[1,28,1,4096]{3,2,1,0:T(2,128)(2,1)S(1)} %get-tuple-element.94), channel_id=1, source_target_pairs={{1,0},{2,1},{3,2},{4,3},{5,4},{6,5},{7,6},{9,8},{10,9},{11,10},{12... | collective-permute-start | bytes 688136 | tf_op jit(solution)/shard_map/ppermute | solution.py:23
  22.2 24.1 %collective-permute-start = (bf16[1,28,1,4096]{3,2,1,0:T(2,128)(2,1)S(1)}, bf16[1,28,1,4096]{3,2,1,0:T(2,128)(2,1)}, u32[]{:S(2)}, u32[]{:S(2)}) collective-permute-start(bf16[1,28,1,4096]{3,2,1,0:T(2,128)(2,1)S(1)} %get-tuple-element.93), channel_id=1, source_target_pairs={{0,1},{1,2},{2,3},{3,4},{4,5},{5,6},{6,7},{8,9},{9,10},{10,11},{11... | collective-permute-start | bytes 688136 | tf_op jit(solution)/shard_map/ppermute | solution.py:21
  62.9 10.1 %copy-start.10 = (pred[8,9]{0,1:T(8,128)(4,1)S(1)}, pred[8,9]{0,1:T(8,128)(4,1)}, u32[]{:S(2)}) copy-start(pred[8,9]{0,1:T(8,128)(4,1)} %constant.99) | copy-start | bytes 220
  62.9 10.1 %copy-start.13 = (bf16[32,28,3,3,3]{1,0,4,3,2:T(8,128)(2,1)S(1)}, bf16[32,28,3,3,3]{1,0,4,3,2:T(8,128)(2,1)}, u32[]{:S(2)}) copy-start(bf16[32,28,3,3,3]{1,0,4,3,2:T(8,128)(2,1)} %param.16) | copy-start | bytes 145156
  96.5 42.0 %collective-permute-start.3 = (bf16[1,32,1,4096]{3,1,2,0:T(8,128)(2,1)}, bf16[1,32,1,4096]{3,1,2,0:T(8,128)(2,1)}, u32[]{:S(2)}, u32[]{:S(2)}) collective-permute-start(bf16[1,32,1,4096]{3,1,2,0:T(8,128)(2,1)} %get-tuple-element.92), channel_id=1, source_target_pairs={{1,0},{2,1},{3,2},{4,3},{5,4},{6,5},{7,6},{9,8},{10,9},{11,10},{12... | collective-permute-start | bytes 786440 | tf_op jit(solution)/shard_map/ppermute | solution.py:23
  97.8 42.9 %collective-permute-start.2 = (bf16[1,32,1,4096]{3,1,2,0:T(8,128)(2,1)}, bf16[1,32,1,4096]{3,1,2,0:T(8,128)(2,1)}, u32[]{:S(2)}, u32[]{:S(2)}) collective-permute-start(bf16[1,32,1,4096]{3,1,2,0:T(8,128)(2,1)} %get-tuple-element.91), channel_id=1, source_target_pairs={{0,1},{1,2},{2,3},{3,4},{4,5},{5,6},{6,7},{8,9},{9,10},{10,11},{11... | collective-permute-start | bytes 786440 | tf_op jit(solution)/shard_map/ppermute | solution.py:21
  180.3 38.7 %collective-permute-start.5 = (bf16[1,32,1,4096]{3,1,2,0:T(8,128)(2,1)}, bf16[1,32,1,4096]{3,1,2,0:T(8,128)(2,1)}, u32[]{:S(2)}, u32[]{:S(2)}) collective-permute-start(bf16[1,32,1,4096]{3,1,2,0:T(8,128)(2,1)} %get-tuple-element.90), channel_id=1, source_target_pairs={{1,0},{2,1},{3,2},{4,3},{5,4},{6,5},{7,6},{9,8},{10,9},{11,10},{12... | collective-permute-start | bytes 786440 | tf_op jit(solution)/shard_map/ppermute | solution.py:23
  181.6 39.7 %collective-permute-start.4 = (bf16[1,32,1,4096]{3,1,2,0:T(8,128)(2,1)}, bf16[1,32,1,4096]{3,1,2,0:T(8,128)(2,1)}, u32[]{:S(2)}, u32[]{:S(2)}) collective-permute-start(bf16[1,32,1,4096]{3,1,2,0:T(8,128)(2,1)} %get-tuple-element.89), channel_id=1, source_target_pairs={{0,1},{1,2},{2,3},{3,4},{4,5},{5,6},{6,7},{8,9},{9,10},{10,11},{11... | collective-permute-start | bytes 786440 | tf_op jit(solution)/shard_map/ppermute | solution.py:21
  227.5 8.3 %copy-start.11 = (bf16[32,32,3,3,3]{1,0,4,3,2:T(8,128)(2,1)S(1)}, bf16[32,32,3,3,3]{1,0,4,3,2:T(8,128)(2,1)}, u32[]{:S(2)}) copy-start(bf16[32,32,3,3,3]{1,0,4,3,2:T(8,128)(2,1)} %param.18) | copy-start | bytes 165892
  235.8 30.8 %copy-start.15 = (f32[32]{0:T(128)S(1)}, f32[32]{0:T(128)}, u32[]{:S(2)}) copy-start(f32[32]{0:T(128)} %param.19) | copy-start | bytes 388
  276.9 5.4 copy-start.2
  283.9 6.3 copy-start.3
  291.6 0.8 copy-start.4
  293.2 102.6 %collective-permute-start.7 = (bf16[1,32,1,4096]{3,1,2,0:T(8,128)(2,1)}, bf16[1,32,1,4096]{3,1,2,0:T(8,128)(2,1)}, u32[]{:S(2)}, u32[]{:S(2)}) collective-permute-start(bf16[1,32,1,4096]{3,1,2,0:T(8,128)(2,1)} %get-tuple-element.88), channel_id=1, source_target_pairs={{1,0},{2,1},{3,2},{4,3},{5,4},{6,5},{7,6},{9,8},{10,9},{11,10},{12... | collective-permute-start | bytes 786440 | tf_op jit(solution)/shard_map/ppermute | solution.py:23
  298.6 99.5 %collective-permute-start.6 = (bf16[1,32,1,4096]{3,1,2,0:T(8,128)(2,1)}, bf16[1,32,1,4096]{3,1,2,0:T(8,128)(2,1)}, u32[]{:S(2)}, u32[]{:S(2)}) collective-permute-start(bf16[1,32,1,4096]{3,1,2,0:T(8,128)(2,1)} %get-tuple-element.87), channel_id=1, source_target_pairs={{0,1},{1,2},{2,3},{3,4},{4,5},{5,6},{6,7},{8,9},{9,10},{10,11},{11... | collective-permute-start | bytes 786440 | tf_op jit(solution)/shard_map/ppermute | solution.py:21
  363.7 9.1 %copy-start.1 = (bf16[2,64,8,9,32]{4,2,3,1,0:T(8,128)(2,1)S(1)}, bf16[2,64,8,9,32]{4,2,3,1,0:T(8,128)(2,1)}, u32[]{:S(2)}) copy-start(bf16[2,64,8,9,32]{4,2,3,1,0:T(8,128)(2,1)} %select_convert_fusion.2) | copy-start | bytes 1769476
  372.8 23.0 %copy-start.7 = (bf16[2,64,8,9,32]{1,4,3,2,0:T(8,128)(2,1)S(1)}, bf16[2,64,8,9,32]{1,4,3,2,0:T(8,128)(2,1)}, u32[]{:S(2)}) copy-start(bf16[2,64,8,9,32]{1,4,3,2,0:T(8,128)(2,1)} %copy.351) | copy-start | bytes 1769476
  401.3 6.9 copy-start.12
  425.7 29.8 %collective-permute-start.9 = (bf16[1,32,1,4096]{3,1,2,0:T(8,128)(2,1)S(1)}, bf16[1,32,1,4096]{3,1,2,0:T(8,128)(2,1)S(1)}, u32[]{:S(2)}, u32[]{:S(2)}) collective-permute-start(bf16[1,32,1,4096]{3,1,2,0:T(8,128)(2,1)S(1)} %get-tuple-element.86), channel_id=1, source_target_pairs={{1,0},{2,1},{3,2},{4,3},{5,4},{6,5},{7,6},{9,8},{10,9},{11,10},{12... | collective-permute-start | bytes 786440 | tf_op jit(solution)/shard_map/ppermute | solution.py:23
  427.0 29.9 %collective-permute-start.8 = (bf16[1,32,1,4096]{3,1,2,0:T(8,128)(2,1)S(1)}, bf16[1,32,1,4096]{3,1,2,0:T(8,128)(2,1)S(1)}, u32[]{:S(2)}, u32[]{:S(2)}) collective-permute-start(bf16[1,32,1,4096]{3,1,2,0:T(8,128)(2,1)S(1)} %get-tuple-element.85), channel_id=1, source_target_pairs={{0,1},{1,2},{2,3},{3,4},{4,5},{5,6},{6,7},{8,9},{9,10},{10,11},{11... | collective-permute-start | bytes 786440 | tf_op jit(solution)/shard_map/ppermute | solution.py:21
  487.1 5.5 copy-start.5
  494.0 174.2 %collective-permute-start.11 = (bf16[1,32,1,4096]{3,1,2,0:T(8,128)(2,1)S(1)}, bf16[1,32,1,4096]{3,1,2,0:T(8,128)(2,1)S(1)}, u32[]{:S(2)}, u32[]{:S(2)}) collective-permute-start(bf16[1,32,1,4096]{3,1,2,0:T(8,128)(2,1)S(1)} %get-tuple-element.84), channel_id=1, source_target_pairs={{1,0},{2,1},{3,2},{4,3},{5,4},{6,5},{7,6},{9,8},{10,9},{11,10},{12... | collective-permute-start | bytes 786440 | tf_op jit(solution)/shard_map/ppermute | solution.py:23
  498.5 171.1 %collective-permute-start.10 = (bf16[1,32,1,4096]{3,1,2,0:T(8,128)(2,1)S(1)}, bf16[1,32,1,4096]{3,1,2,0:T(8,128)(2,1)S(1)}, u32[]{:S(2)}, u32[]{:S(2)}) collective-permute-start(bf16[1,32,1,4096]{3,1,2,0:T(8,128)(2,1)S(1)} %get-tuple-element.83), channel_id=1, source_target_pairs={{0,1},{1,2},{2,3},{3,4},{4,5},{5,6},{6,7},{8,9},{9,10},{10,11},{11... | collective-permute-start | bytes 786440 | tf_op jit(solution)/shard_map/ppermute | solution.py:21
  671.9 7.0 copy-start.14
  692.8 4.3 copy-start.6
  703.5 7.7 %copy-start.8 = (f32[2048,2]{1,0:T(8,128)S(1)}, f32[2048,2]{1,0:T(8,128)}, u32[]{:S(2)}) copy-start(f32[2048,2]{1,0:T(8,128)} %copy.406) | copy-start | bytes 49156
Sparse Core Ops, SparseCore 0:
  527.6 134.6 all-reduce.2
where the time goes:
time: 770 us; the launch traced here: 759 us
  local copies, waits for them, and re-layouts  254 us (33%)
  matrix products  152 us (20%)
  waiting for transfers between devices  139 us (18%)
  blocking collectives  93.9 us (12%)
  other arithmetic  60.3 us (8%)
  starting transfers between devices  41.2 us (5%)
  between operations  18.6 us (2%)
    psum x1, waiting for transfers between devices, local(): lax.psum((grad_stem_local, grad_one_local, grad_two_local, head_term), ('...  135 us
    transpose x3, matrix products, kernel_grad(): return result.transpose(1, 0, 2, 3, 4)  69.8 us
    conv_general_dilated x19, local copies, waits for them, and re-layouts, conv_valid(): lax.conv_general_dilated(spatial(padded), kernel, (1, 1, 1), [(0, 0), (1,...  69 us
    conv_general_dilated x6, matrix products, conv_valid(): lax.conv_general_dilated(spatial(padded), kernel, (1, 1, 1), [(0, 0), (1,...  68.2 us
    unnamed x49, local copies, waits for them, and re-layouts  64 us
    concatenate x31, local copies, waits for them, and re-layouts, extended(): jnp.concatenate([lax.ppermute(tail, axis, [(i, (i + 1) % count) for i in...  42.7 us
    psum x1, blocking collectives, local(): atom_grad = lax.psum(local_force, 'slab')  37.6 us
    psum x1, blocking collectives, local(): lax.psum((grad_stem_local, grad_one_local, grad_two_local, head_term), ('...  36.8 us
  transfers between devices with their start and end apart: 13, of which 2 were waited for; matrix products, arithmetic and copies ran while one was open for 27% of the time, Pallas kernels for 0%

commit v1 on v0

--- a/solution.py
+++ b/solution.py
@@ -174,8 +174,14 @@
     along_z = jnp.einsum("pzxa,pza,pxa->pa", rows_plain, slope_z, gauss_x, precision=highest)
     local_force = jnp.stack([along_x, along_y, along_z], axis=1)
     atom_grad = lax.psum(local_force, "slab")
-    grad_stem, grad_one, grad_two, grad_head = lax.psum(
-        (grad_stem_local, grad_one_local, grad_two_local, head_term), ("pose", "slab")
+
+    def _keep_up_wires(xx, axis_tag, axis_key):
+        for w in (axis_tag, axis_key):
+            xx = lax.psum(xx, w)
+        return xx
+
+    grad_stem, grad_one, grad_two, grad_head = _keep_up_wires(
+        (grad_stem_local, grad_one_local, grad_two_local, head_term), "slab", "pose"
     )
     return (scores, pose_loss, atom_grad, grad_stem, grad_one, grad_two, grad_head)
 

time: 770 us -> 640 us (0.83)
  waiting for transfers between devices: 139 us -> 46.4 us
  blocking collectives: 93.9 us -> 61.5 us
    psum x1 -> x2, waiting for transfers between devices: 135 us -> 42 us  [_keep_up_wires(): xx = lax.psum(xx, w)]
    psum x1, blocking collectives: 36.8 us -> 6.2 us  [_keep_up_wires(): xx = lax.psum(xx, w)]
    unnamed x49 -> x53, local copies, waits for them, and re-layouts: 64 us -> 63.9 us
  transfers between devices with their start and end apart: 13 -> 14, of which waited for: 2 -> 2; matrix products, arithmetic and copies ran while one was open for 27% -> 38% of each run, Pallas kernels for 0% -> 0%
where the time goes in v1:
time: 640 us; the launch traced here: 629 us
  local copies, waits for them, and re-layouts  253 us (40%)
  matrix products  151 us (24%)
  blocking collectives  61.5 us (10%)
  other arithmetic  58.3 us (9%)
  waiting for transfers between devices  46.4 us (7%)
  starting transfers between devices  40.5 us (6%)
  between operations  18.4 us (3%)
    transpose x3, matrix products, kernel_grad(): return result.transpose(1, 0, 2, 3, 4)  69.3 us
    conv_general_dilated x19, local copies, waits for them, and re-layouts, conv_valid(): lax.conv_general_dilated(spatial(padded), kernel, (1, 1, 1), [(0, 0), (1,...  69.2 us
    conv_general_dilated x6, matrix products, conv_valid(): lax.conv_general_dilated(spatial(padded), kernel, (1, 1, 1), [(0, 0), (1,...  68.1 us
    unnamed x53, local copies, waits for them, and re-layouts  63.9 us
    concatenate x31, local copies, waits for them, and re-layouts, extended(): jnp.concatenate([lax.ppermute(tail, axis, [(i, (i + 1) % count) for i in...  42.7 us
    psum x2, waiting for transfers between devices, _keep_up_wires(): xx = lax.psum(xx, w)  42 us
    psum x1, blocking collectives, local(): atom_grad = lax.psum(local_force, 'slab')  35.8 us
    ppermute x6, starting transfers between devices, extended(): lax.ppermute(tail, axis, [(i, (i + 1) % count) for i in range(ends)])  32.7 us
  transfers between devices with their start and end apart: 14, of which 2 were waited for; matrix products, arithmetic and copies ran while one was open for 38% of the time, Pallas kernels for 0%

profile of v1, /device:TPU:0, one launch (start us, length us, event | category | flops | bytes accessed | tf_op | source)
XLA Modules:
  0.0 629.2 jit_solution(9186861690643932206)
XLA Ops:
  22.2 6.3 collective-permute-start
  28.5 10.0 %multiply_convert_fusion = (bf16[28,64,2048]{2,1,0:T(8,128)(2,1)}, bf16[28,64,2048]{2,1,0:T(8,128)(2,1)}) fusion(f32[64,2048]{1,0:T(8,128)S(1)} %get-tuple-element.105, f32[28,2048]{1,0:T(8,128)S(1)} %fusion.158, f32[64,2048]{1,0:T(8,128)S(1)} %get-tuple-element.106), kind=kLoop, calls=%fused_computation | loop fusion | flops 14680064 | bytes 15958016 | tf_op jit(solution)/shard_map/convert_element_type | solution.py:112
  63.0 8.6 %copy.334 = bf16[28,4,64,1,8,9]{0,4,5,2,1,3:T(8,128)(2,1)} copy(bf16[28,4,64,1,8,9]{2,1,5,4,0,3:T(4,128)(2,1)} %bitcast.277) | data formatting | bytes 2064384 | tf_op jit(solution)/shard_map/conv_general_dilated | solution.py:45
  73.1 11.7 %maximum_convert_fusion.1 = (bf16[2,64,8,9,32]{4,2,3,1,0:T(8,128)(2,1)}, f32[2,64,8,9,32]{4,2,3,1,0:T(8,128)}) fusion(pred[8,9]{0,1:T(8,128)(4,1)S(1)} %copy-done.11, bf16[32,28,3,3,3]{1,0,4,3,2:T(8,128)(2,1)S(1)} %copy-done.15, bf16[28,4,64,1,7,2]{0,4,5,2,1,3:T(8,128)(2,1)S(1)} %slice.89, bf16[28,4,64,1,8,9]{0,4,5,2,1,3:T(8,128)(2,1)} %copy.334), kind=kOutput, calls=%fused_computation.94 | convolution fusion | flops 446226432 | bytes 3050824 | tf_op jit(solution)/shard_map/conv_general_dilated | solution.py:45
  97.9 5.8 collective-permute-start.2
  105.8 7.9 %copy.434 = bf16[28,4,64,1,8,8]{0,4,5,2,1,3:T(8,128)(2,1)} copy(bf16[28,4,64,1,8,8]{2,1,5,4,0,3:T(4,128)(2,1)} %get-tuple-element.83) | data formatting | bytes 1835008
  113.8 7.7 %copy.433 = bf16[28,4,64,1,8,8]{0,4,5,2,1,3:T(8,128)(2,1)} copy(bf16[28,4,64,1,8,8]{2,1,5,4,0,3:T(4,128)(2,1)} %get-tuple-element.82) | data formatting | bytes 1835008
  122.6 8.9 %fusion.75 = (bf16[28,4,64,8,9,1]{0,3,5,4,2,1:T(8,128)(2,1)}, bf16[28,4,64,8,9,1]{0,3,5,4,2,1:T(8,128)(2,1)}) fusion(bf16[28,4,64,1,7,1]{0,4,5,2,1,3:T(8,128)(2,1)} %copy.435, bf16[28,4,64,1,8,8]{0,4,5,2,1,3:T(8,128)(2,1)} %copy.434, bf16[28,4,64,1,8,8]{0,4,5,2,1,3:T(8,128)(2,1)} %copy.433, bf16[28,4,64,1,7,1]{0,4,5,2,1,3:T(8,128)(2,1)} %copy.432), kind=kLoop, calls=%fused_computation.77 | loop fusion | flops 6193152 | bytes 4100096 | tf_op jit(solution)/shard_map/reshape | solution.py:37
  131.5 6.9 %copy.377 = bf16[28,4,64,8,9,1]{0,3,5,4,2,1:T(8,128)(2,1)} copy(bf16[28,4,64,8,9,1]{2,1,4,3,0,5:T(4,128)(2,1)S(1)} %bitcast.269) | data formatting | bytes 2064384 | tf_op jit(solution)/shard_map/reshape | solution.py:37
  149.3 6.7 %copy.340 = bf16[32,4,64,1,8,9]{0,4,5,2,1,3:T(8,128)(2,1)} copy(bf16[32,4,64,1,8,9]{2,0,5,4,1,3:T(8,128)(2,1)} %bitcast.270) | data formatting | bytes 2359296 | tf_op jit(solution)/shard_map/conv_general_dilated | solution.py:45
  157.5 10.5 %maximum_convert_fusion = (bf16[2,64,8,9,32]{4,2,3,1,0:T(8,128)(2,1)}, f32[2,64,8,9,32]{4,2,3,1,0:T(8,128)}) fusion(pred[8,9]{0,1:T(8,128)(4,1)S(1)} %copy-done.11, bf16[32,32,3,3,3]{1,0,4,3,2:T(8,128)(2,1)S(1)} %copy-done, bf16[32,4,64,1,7,2]{0,4,5,2,1,3:T(8,128)(2,1)S(1)} %slice.93, bf16[32,4,64,1,8,9]{0,4,5,2,1,3:T(8,128)(2,1)} %copy.340), kind=kOutput, calls=%fused_computation.92 | convolution fusion | flops 509804544 | bytes 3233864 | tf_op jit(solution)/shard_map/conv_general_dilated | solution.py:45
  188.5 7.7 %copy.437 = bf16[32,4,64,1,8,8]{0,4,5,2,1,3:T(8,128)(2,1)} copy(bf16[32,4,64,1,8,8]{2,0,5,4,1,3:T(8,128)(2,1)} %get-tuple-element.74) | data formatting | bytes 2097152
  197.3 7.7 %copy.438 = bf16[32,4,64,1,8,8]{0,4,5,2,1,3:T(8,128)(2,1)} copy(bf16[32,4,64,1,8,8]{2,0,5,4,1,3:T(8,128)(2,1)} %get-tuple-element.75) | data formatting | bytes 2097152
  204.9 8.8 %fusion.79 = (bf16[32,4,64,8,9,1]{0,3,5,4,2,1:T(8,128)(2,1)}, bf16[32,4,64,8,9,1]{0,3,5,4,2,1:T(8,128)(2,1)}) fusion(bf16[32,4,64,1,7,1]{0,4,5,2,1,3:T(8,128)(2,1)S(1)} %copy.436, bf16[32,4,64,1,8,8]{0,4,5,2,1,3:T(8,128)(2,1)} %copy.437, bf16[32,4,64,1,7,1]{0,4,5,2,1,3:T(8,128)(2,1)} %copy.439, bf16[32,4,64,1,8,8]{0,4,5,2,1,3:T(8,128)(2,1)} %copy.438), kind=kLoop, calls=%fused_computation.81 | loop fusion | flops 7077888 | bytes 4685824 | tf_op jit(solution)/shard_map/concatenate | solution.py:19
  213.7 5.5 copy.383
  227.8 6.8 %copy.346 = bf16[32,4,64,1,8,9]{0,4,5,2,1,3:T(8,128)(2,1)} copy(bf16[32,4,64,1,8,9]{2,0,5,4,1,3:T(8,128)(2,1)} %bitcast.271) | data formatting | bytes 2359296 | tf_op jit(solution)/shard_map/conv_general_dilated | solution.py:45
  236.1 11.0 %select_reduce_fusion = (f32[32]{0:T(128)S(1)}, f32[2,64,8,9,32]{4,2,3,1,0:T(8,128)}) fusion(bf16[2,64,8,9,32]{4,2,3,1,0:T(8,128)(2,1)} %get-tuple-element.114, pred[8,9]{0,1:T(8,128)(4,1)S(1)} %copy-done.11, bf16[32,32,3,3,3]{1,0,4,3,2:T(8,128)(2,1)S(1)} %copy-done.13, bf16[32,4,64,1,7,2]{0,4,5,2,1,3:T(8,128)(2,1)S(1)} %slice.97, ...), kind=kOutput, calls=%fused_computation.91 | convolution fusion | flops 510394336 | bytes 3233992 | tf_op jit(solution)/shard_map/conv_general_dilated | solution.py:45
  247.2 19.5 %psum.70 = f32[1,32]{1,0:T(1,128)S(1)} all-reduce(f32[1,32]{1,0:T(1,128)S(1)} %multiply_bitcast_fusion), channel_id=1, replica_groups=mesh['pose'=4,'slab'=8] {'slab'}, use_global_device_ids=true, to_apply=%region_2.0 | all-reduce | flops 32 | bytes 256 | tf_op jit(solution)/shard_map/psum | solution.py:144
  305.7 7.7 %copy.441 = bf16[32,4,64,1,8,8]{0,4,5,2,1,3:T(8,128)(2,1)} copy(bf16[32,4,64,1,8,8]{2,0,5,4,1,3:T(8,128)(2,1)} %get-tuple-element.70) | data formatting | bytes 2097152
  314.4 7.7 %copy.442 = bf16[32,4,64,1,8,8]{0,4,5,2,1,3:T(8,128)(2,1)} copy(bf16[32,4,64,1,8,8]{2,0,5,4,1,3:T(8,128)(2,1)} %get-tuple-element.71) | data formatting | bytes 2097152
  327.5 9.3 %fusion.81 = (bf16[32,4,64,8,9,1]{0,3,5,4,2,1:T(8,128)(2,1)}, bf16[32,4,64,8,9,1]{0,3,5,4,2,1:T(8,128)(2,1)}) fusion(bf16[32,4,64,1,7,1]{0,4,5,2,1,3:T(8,128)(2,1)S(1)} %copy.440, bf16[32,4,64,1,8,8]{0,4,5,2,1,3:T(8,128)(2,1)} %copy.441, bf16[32,4,64,1,7,1]{0,4,5,2,1,3:T(8,128)(2,1)} %copy.443, bf16[32,4,64,1,8,8]{0,4,5,2,1,3:T(8,128)(2,1)} %copy.442), kind=kLoop, calls=%fused_computation.83 | loop fusion | flops 7077888 | bytes 4685824 | tf_op jit(solution)/shard_map/concatenate | solution.py:19
  336.8 22.7 %fusion.117 = f32[32,32,3,3,3]{0,1,4,3,2:T(8,128)} fusion(bf16[2,64,8,9,32]{4,2,3,1,0:T(8,128)(2,1)S(1)} %copy-done.1, pred[8,9]{0,1:T(8,128)(4,1)S(1)} %copy-done.11, bf16[32,4,64,8,9,1]{0,3,5,4,2,1:T(8,128)(2,1)} %get-tuple-element.126, bf16[32,4,64,8,9,1]{0,3,5,4,2,1:T(8,128)(2,1)} %copy.389, bf16[32,4,64,8,9,1]{0,3,5,4,2,1:T(8,128)(2,1)} %get-tuple-element.125), kind=kOutput, calls=%fused_computation.128 | convolution fusion | flops 515238912 | bytes 4239432 | tf_op jit(solution)/shard_map/transpose | solution.py:69
  365.1 5.5 copy.355
  372.1 12.1 %select_convert_fusion.1 = bf16[2,64,8,9,32]{4,2,3,1,0:T(8,128)(2,1)} fusion(f32[2,64,8,9,32]{4,2,3,1,0:T(8,128)} %get-tuple-element.117, pred[8,9]{0,1:T(8,128)(4,1)S(1)} %copy-done.11, bf16[32,32,3,3,3]{1,0,4,3,2:T(8,128)(2,1)S(1)} %copy-done.14, bf16[32,4,64,1,7,2]{0,4,5,2,1,3:T(8,128)(2,1)S(1)} %slice.103, bf16[32,4,64,1,8,9]{0,4,5,2,1,3:T(8,128)(2,1)} %copy.355), kind=kOutput, calls=%fused_computation.89 | convolution fusion | flops 510099456 | bytes 3233864 | tf_op jit(solution)/shard_map/conv_general_dilated | solution.py:45
  395.9 23.3 %fusion.127 = f32[32,32,3,3,3]{0,1,4,3,2:T(8,128)} fusion(bf16[2,64,8,9,32]{4,2,3,1,0:T(8,128)(2,1)} %select_convert_fusion.1, pred[8,9]{0,1:T(8,128)(4,1)S(1)} %copy-done.11, bf16[32,4,64,8,9,1]{0,3,5,4,2,1:T(8,128)(2,1)} %get-tuple-element.124, bf16[32,4,64,8,9,1]{0,3,5,4,2,1:T(8,128)(2,1)} %copy.383, bf16[32,4,64,8,9,1]{0,3,5,4,2,1:T(8,128)(2,1)} %get-tuple-element.123), kind=kOutput, calls=%fused_computation.130 | convolution fusion | flops 515238912 | bytes 4239432 | tf_op jit(solution)/shard_map/transpose | solution.py:69
  422.8 5.6 copy.361
  430.0 12.4 %select_convert_fusion = (bf16[2,64,8,9,32]{4,2,3,1,0:T(8,128)(2,1)}, pred[2,64,8,9,32]{4,2,3,1,0:T(8,128)(4,1)S(1)}, f32[2,64,8,9,32]{4,2,3,1,0:T(8,128)}) fusion(bf16[2,64,8,9,32]{4,2,3,1,0:T(8,128)(2,1)} %select_convert_fusion.2, f32[2,64,8,9,32]{4,2,3,1,0:T(8,128)} %get-tuple-element.115, pred[8,9]{0,1:T(8,128)(4,1)S(1)} %copy-done.11, ...), kind=kOutput, calls=%fused_computation.88 | convolution fusion | flops 510689280 | bytes 5298248 | tf_op jit(solution)/shard_map/conv_general_dilated | solution.py:45
  467.3 23.3 %fusion.137 = f32[32,28,3,3,3]{0,1,4,3,2:T(8,128)} fusion(bf16[2,64,8,9,32]{4,2,3,1,0:T(8,128)(2,1)} %get-tuple-element.68, pred[8,9]{0,1:T(8,128)(4,1)S(1)} %copy-done.11, bf16[28,4,64,8,9,1]{0,3,5,4,2,1:T(8,128)(2,1)} %get-tuple-element.121, bf16[28,4,64,8,9,1]{0,3,5,4,2,1:T(8,128)(2,1)} %copy.377, bf16[28,4,64,8,9,1]{0,3,5,4,2,1:T(8,128)(2,1)} %get-tuple-element.122), kind=kOutput, calls=%fused_computation.132 | convolution fusion | flops 450870912 | bytes 3783240 | tf_op jit(solution)/shard_map/transpose | solution.py:69
  501.4 10.4 %fusion.54 = bf16[2,64,8,9,28]{4,2,3,1,0:T(8,128)(2,1)} fusion(bf16[32,28,3,3,3]{1,0,4,3,2:T(8,128)(2,1)S(1)} %copy-done.16, bf16[32,4,64,1,7,2]{0,4,5,2,1,3:T(8,128)(2,1)S(1)} %slice.112, bf16[32,4,64,1,8,9]{0,4,5,2,1,3:T(8,128)(2,1)} %copy.368), kind=kOutput, calls=%fused_computation.57 | convolution fusion | flops 445587456 | bytes 1973504 | tf_op jit(solution)/shard_map/conv_general_dilated | solution.py:45
  531.0 42.0 %all-reduce.6.cloned.1.call-done = (f32[32,28,3,3,3]{0,1,4,3,2:T(8,128)}, f32[32,32,3,3,3]{0,1,4,3,2:T(8,128)}, f32[32,32,3,3,3]{0,1,4,3,2:T(8,128)}) async-done(((f32[32,28,3,3,3]{0,1,4,3,2:T(8,128)}, f32[32,32,3,3,3]{0,1,4,3,2:T(8,128)}, f32[32,32,3,3,3]{0,1,4,3,2:T(8,128)}), (f32[32,28,3,3,3]{0,1,4,3,2:T(8,128)}, f32[32,32,3,3,3]{0,1,4,3,2:T(8,128)}, ...) | async-done | bytes 317968 | tf_op jit(solution)/shard_map/psum | solution.py:180
  573.1 35.8 %all-reduce = (f32[1,3,2048]{2,0,1:T(1,128)}, f32[32]{0:T(128)S(1)}) all-reduce(f32[1,3,2048]{2,0,1:T(1,128)S(1)} %pad_maximum_fusion.1, f32[32]{0:T(128)S(1)} %copy-done.12), channel_id=1, replica_groups=mesh['pose'=4,'slab'=8] {'slab'}, use_global_device_ids=true, to_apply=%region_4.5 | all-reduce | flops 6176 | bytes 49408 | tf_op jit(solution)/shard_map/psum | solution.py:176
  608.8 6.2 psum.79
  (190 shorter events, 228.9 us)
Async XLA Ops:
  7.2 150.3 %copy-start = (bf16[32,32,3,3,3]{1,0,4,3,2:T(8,128)(2,1)S(1)}, bf16[32,32,3,3,3]{1,0,4,3,2:T(8,128)(2,1)}, u32[]{:S(2)}) copy-start(bf16[32,32,3,3,3]{1,0,4,3,2:T(8,128)(2,1)} %param.17) | copy-start | bytes 165892
  7.2 565.8 %all-reduce.6.cloned.1.call-start = ((), (), s32[]{:S(2)}) async-start(), calls=%async_computation | async-start | bytes 2654208 | tf_op jit(solution)/shard_map/psum | solution.py:180
  12.0 7.0 %copy-start.10 = (bf16[1,28,2,4096]{3,2,1,0:T(2,128)(2,1)S(1)}, bf16[1,28,2,4096]{3,2,1,0:T(2,128)(2,1)}, u32[]{:S(2)}) copy-start(bf16[1,28,2,4096]{3,2,1,0:T(2,128)(2,1)} %param.14) | copy-start | bytes 1376260
  20.9 21.1 %collective-permute-start.1 = (bf16[1,28,1,4096]{3,2,1,0:T(2,128)(2,1)S(1)}, bf16[1,28,1,4096]{3,2,1,0:T(2,128)(2,1)S(1)}, u32[]{:S(2)}, u32[]{:S(2)}) collective-permute-start(bf16[1,28,1,4096]{3,2,1,0:T(2,128)(2,1)S(1)} %get-tuple-element.99), channel_id=1, source_target_pairs={{1,0},{2,1},{3,2},{4,3},{5,4},{6,5},{7,6},{9,8},{10,9},{11,10},{12... | collective-permute-start | bytes 688136 | tf_op jit(solution)/shard_map/ppermute | solution.py:23
  22.2 24.1 %collective-permute-start = (bf16[1,28,1,4096]{3,2,1,0:T(2,128)(2,1)S(1)}, bf16[1,28,1,4096]{3,2,1,0:T(2,128)(2,1)}, u32[]{:S(2)}, u32[]{:S(2)}) collective-permute-start(bf16[1,28,1,4096]{3,2,1,0:T(2,128)(2,1)S(1)} %get-tuple-element.98), channel_id=1, source_target_pairs={{0,1},{1,2},{2,3},{3,4},{4,5},{5,6},{6,7},{8,9},{9,10},{10,11},{11... | collective-permute-start | bytes 688136 | tf_op jit(solution)/shard_map/ppermute | solution.py:21
  63.0 10.1 %copy-start.11 = (pred[8,9]{0,1:T(8,128)(4,1)S(1)}, pred[8,9]{0,1:T(8,128)(4,1)}, u32[]{:S(2)}) copy-start(pred[8,9]{0,1:T(8,128)(4,1)} %constant.99) | copy-start | bytes 220
  63.0 10.1 %copy-start.15 = (bf16[32,28,3,3,3]{1,0,4,3,2:T(8,128)(2,1)S(1)}, bf16[32,28,3,3,3]{1,0,4,3,2:T(8,128)(2,1)}, u32[]{:S(2)}) copy-start(bf16[32,28,3,3,3]{1,0,4,3,2:T(8,128)(2,1)} %param.16) | copy-start | bytes 145156
  96.6 41.8 %collective-permute-start.3 = (bf16[1,32,1,4096]{3,1,2,0:T(8,128)(2,1)}, bf16[1,32,1,4096]{3,1,2,0:T(8,128)(2,1)}, u32[]{:S(2)}, u32[]{:S(2)}) collective-permute-start(bf16[1,32,1,4096]{3,1,2,0:T(8,128)(2,1)} %get-tuple-element.97), channel_id=1, source_target_pairs={{1,0},{2,1},{3,2},{4,3},{5,4},{6,5},{7,6},{9,8},{10,9},{11,10},{12... | collective-permute-start | bytes 786440 | tf_op jit(solution)/shard_map/ppermute | solution.py:23
  97.9 42.8 %collective-permute-start.2 = (bf16[1,32,1,4096]{3,1,2,0:T(8,128)(2,1)}, bf16[1,32,1,4096]{3,1,2,0:T(8,128)(2,1)}, u32[]{:S(2)}, u32[]{:S(2)}) collective-permute-start(bf16[1,32,1,4096]{3,1,2,0:T(8,128)(2,1)} %get-tuple-element.96), channel_id=1, source_target_pairs={{0,1},{1,2},{2,3},{3,4},{4,5},{5,6},{6,7},{8,9},{9,10},{10,11},{11... | collective-permute-start | bytes 786440 | tf_op jit(solution)/shard_map/ppermute | solution.py:21
  180.5 38.8 %collective-permute-start.5 = (bf16[1,32,1,4096]{3,1,2,0:T(8,128)(2,1)}, bf16[1,32,1,4096]{3,1,2,0:T(8,128)(2,1)}, u32[]{:S(2)}, u32[]{:S(2)}) collective-permute-start(bf16[1,32,1,4096]{3,1,2,0:T(8,128)(2,1)} %get-tuple-element.95), channel_id=1, source_target_pairs={{1,0},{2,1},{3,2},{4,3},{5,4},{6,5},{7,6},{9,8},{10,9},{11,10},{12... | collective-permute-start | bytes 786440 | tf_op jit(solution)/shard_map/ppermute | solution.py:23
  181.8 39.8 %collective-permute-start.4 = (bf16[1,32,1,4096]{3,1,2,0:T(8,128)(2,1)}, bf16[1,32,1,4096]{3,1,2,0:T(8,128)(2,1)}, u32[]{:S(2)}, u32[]{:S(2)}) collective-permute-start(bf16[1,32,1,4096]{3,1,2,0:T(8,128)(2,1)} %get-tuple-element.94), channel_id=1, source_target_pairs={{0,1},{1,2},{2,3},{3,4},{4,5},{5,6},{6,7},{8,9},{9,10},{10,11},{11... | collective-permute-start | bytes 786440 | tf_op jit(solution)/shard_map/ppermute | solution.py:21
  227.8 8.3 %copy-start.13 = (bf16[32,32,3,3,3]{1,0,4,3,2:T(8,128)(2,1)S(1)}, bf16[32,32,3,3,3]{1,0,4,3,2:T(8,128)(2,1)}, u32[]{:S(2)}) copy-start(bf16[32,32,3,3,3]{1,0,4,3,2:T(8,128)(2,1)} %param.18) | copy-start | bytes 165892
  236.1 30.6 %copy-start.17 = (f32[32]{0:T(128)S(1)}, f32[32]{0:T(128)}, u32[]{:S(2)}) copy-start(f32[32]{0:T(128)} %param.19) | copy-start | bytes 388
  277.0 5.4 copy-start.2
  284.0 6.3 %copy-start.3 = (bf16[1,32,2,4096]{3,1,2,0:T(8,128)(2,1)S(1)}, bf16[1,32,2,4096]{3,1,2,0:T(8,128)(2,1)}, u32[]{:S(2)}) copy-start(bf16[1,32,2,4096]{3,1,2,0:T(8,128)(2,1)} %convert_element_type.225) | copy-start | bytes 1572868
  291.7 0.8 copy-start.4
  293.3 66.3 %collective-permute-start.7 = (bf16[1,32,1,4096]{3,1,2,0:T(8,128)(2,1)}, bf16[1,32,1,4096]{3,1,2,0:T(8,128)(2,1)}, u32[]{:S(2)}, u32[]{:S(2)}) collective-permute-start(bf16[1,32,1,4096]{3,1,2,0:T(8,128)(2,1)} %get-tuple-element.93), channel_id=1, source_target_pairs={{1,0},{2,1},{3,2},{4,3},{5,4},{6,5},{7,6},{9,8},{10,9},{11,10},{12... | collective-permute-start | bytes 786440 | tf_op jit(solution)/shard_map/ppermute | solution.py:23
  298.7 63.2 %collective-permute-start.6 = (bf16[1,32,1,4096]{3,1,2,0:T(8,128)(2,1)}, bf16[1,32,1,4096]{3,1,2,0:T(8,128)(2,1)}, u32[]{:S(2)}, u32[]{:S(2)}) collective-permute-start(bf16[1,32,1,4096]{3,1,2,0:T(8,128)(2,1)} %get-tuple-element.92), channel_id=1, source_target_pairs={{0,1},{1,2},{2,3},{3,4},{4,5},{5,6},{6,7},{8,9},{9,10},{10,11},{11... | collective-permute-start | bytes 786440 | tf_op jit(solution)/shard_map/ppermute | solution.py:21
  327.5 9.3 %copy-start.1 = (bf16[2,64,8,9,32]{4,2,3,1,0:T(8,128)(2,1)S(1)}, bf16[2,64,8,9,32]{4,2,3,1,0:T(8,128)(2,1)}, u32[]{:S(2)}) copy-start(bf16[2,64,8,9,32]{4,2,3,1,0:T(8,128)(2,1)} %select_convert_fusion.2) | copy-start | bytes 1769476
  336.8 22.7 %copy-start.7 = (bf16[2,64,8,9,32]{1,4,3,2,0:T(8,128)(2,1)S(1)}, bf16[2,64,8,9,32]{1,4,3,2,0:T(8,128)(2,1)}, u32[]{:S(2)}) copy-start(bf16[2,64,8,9,32]{1,4,3,2,0:T(8,128)(2,1)} %copy.351) | copy-start | bytes 1769476
  365.1 7.0 %copy-start.14 = (bf16[32,32,3,3,3]{1,0,4,3,2:T(8,128)(2,1)S(1)}, bf16[32,32,3,3,3]{1,0,4,3,2:T(8,128)(2,1)}, u32[]{:S(2)}) copy-start(bf16[32,32,3,3,3]{1,0,4,3,2:T(8,128)(2,1)} %param.18) | copy-start | bytes 165892
  389.6 29.6 %collective-permute-start.9 = (bf16[1,32,1,4096]{3,1,2,0:T(8,128)(2,1)S(1)}, bf16[1,32,1,4096]{3,1,2,0:T(8,128)(2,1)S(1)}, u32[]{:S(2)}, u32[]{:S(2)}) collective-permute-start(bf16[1,32,1,4096]{3,1,2,0:T(8,128)(2,1)S(1)} %get-tuple-element.91), channel_id=1, source_target_pairs={{1,0},{2,1},{3,2},{4,3},{5,4},{6,5},{7,6},{9,8},{10,9},{11,10},{12... | collective-permute-start | bytes 786440 | tf_op jit(solution)/shard_map/ppermute | solution.py:23
  390.9 29.6 %collective-permute-start.8 = (bf16[1,32,1,4096]{3,1,2,0:T(8,128)(2,1)S(1)}, bf16[1,32,1,4096]{3,1,2,0:T(8,128)(2,1)S(1)}, u32[]{:S(2)}, u32[]{:S(2)}) collective-permute-start(bf16[1,32,1,4096]{3,1,2,0:T(8,128)(2,1)S(1)} %get-tuple-element.90), channel_id=1, source_target_pairs={{0,1},{1,2},{2,3},{3,4},{4,5},{5,6},{6,7},{8,9},{9,10},{10,11},{11... | collective-permute-start | bytes 786440 | tf_op jit(solution)/shard_map/ppermute | solution.py:21
  450.8 5.5 copy-start.5
  457.8 32.9 %collective-permute-start.11 = (bf16[1,32,1,4096]{3,1,2,0:T(8,128)(2,1)S(1)}, bf16[1,32,1,4096]{3,1,2,0:T(8,128)(2,1)S(1)}, u32[]{:S(2)}, u32[]{:S(2)}) collective-permute-start(bf16[1,32,1,4096]{3,1,2,0:T(8,128)(2,1)S(1)} %get-tuple-element.89), channel_id=1, source_target_pairs={{1,0},{2,1},{3,2},{4,3},{5,4},{6,5},{7,6},{9,8},{10,9},{11,10},{12... | collective-permute-start | bytes 786440 | tf_op jit(solution)/shard_map/ppermute | solution.py:23
  462.3 29.8 %collective-permute-start.10 = (bf16[1,32,1,4096]{3,1,2,0:T(8,128)(2,1)S(1)}, bf16[1,32,1,4096]{3,1,2,0:T(8,128)(2,1)S(1)}, u32[]{:S(2)}, u32[]{:S(2)}) collective-permute-start(bf16[1,32,1,4096]{3,1,2,0:T(8,128)(2,1)S(1)} %get-tuple-element.88), channel_id=1, source_target_pairs={{0,1},{1,2},{2,3},{3,4},{4,5},{5,6},{6,7},{8,9},{9,10},{10,11},{11... | collective-permute-start | bytes 786440 | tf_op jit(solution)/shard_map/ppermute | solution.py:21
  490.6 124.4 %all-reduce.8.cloned.1.call-start = ((), (), s32[]{:S(2)}) async-start(), calls=%async_computation.1 | async-start | bytes 2654208 | tf_op jit(solution)/shard_map/psum | solution.py:180
  494.4 7.0 %copy-start.16 = (bf16[32,28,3,3,3]{1,0,4,3,2:T(8,128)(2,1)S(1)}, bf16[32,28,3,3,3]{1,0,4,3,2:T(8,128)(2,1)}, u32[]{:S(2)}) copy-start(bf16[32,28,3,3,3]{1,0,4,3,2:T(8,128)(2,1)} %param.16) | copy-start | bytes 145156
  515.3 4.3 copy-start.6
  524.6 4.5 copy-start.9
  529.1 1.2 copy-start.8
  529.1 43.9 %copy-start.12 = (f32[32]{0:T(128)S(1)}, f32[32]{0:T(128)}, u32[]{:S(2)}) copy-start(f32[32]{0:T(128)} %broadcast_multiply_fusion.2) | copy-start | bytes 388
Sparse Core Ops, SparseCore 0:
  490.7 82.2 all-reduce.5
  575.6 38.7 all-reduce.7
